TPU v7x, 32 devices: a whole 2x2x4 slice. The times are simulated.
32 devices in a mesh: tm: 16 (over z, y, core), space: 2 (over x).
Axes of the slice: x: 2, y: 2, z: 4, core: 2. Of those that a mesh axis runs over, the one named last changes fastest.
Arguments:
- cpoint_guess: float32 [16, 3, 32, 1024], P('tm', None, 'space'), may hold values from -6 to 6
- tide_forcing: float32 [128, 3, 32, 1024], P('tm', None, 'space'), may hold values from -4 to 4
- depth: float32 [32, 1024], P('space'), may hold values from 0.5 to 1.5
- drag: float32 [32, 1024], P('space'), may hold values from 0.01 to 0.08
Outputs:
- improved: float32 [128, 3, 32, 1024], P('tm', None, 'space')
- cpoint_residual: float32 [16, 3, 32, 1024], P('tm', None, 'space')
All inputs are finite; a program needn't handle non-finite values.
Results may differ from a plain program's by a relative error of at most 0.0003.
Values sent between devices are 32-bit elements; how exact they have to be, the bound alone decides.
A program may use at most 128 MiB of HBM per device.

v0:
```python
import jax
import jax.numpy as jnp
from jax import lax
from jax.sharding import PartitionSpec as P

LEVELS = 5


coriolis = 0.1
fine_courant = 0.25
coarse_courant = 0.5


def with_halo(cells, sides, width):
    for axis, dim in sides:
        count = lax.axis_size(axis)
        head = lax.slice_in_dim(cells, 0, width, axis=dim)
        tail = lax.slice_in_dim(cells, cells.shape[dim] - width, cells.shape[dim], axis=dim)
        cells = jnp.concatenate(
            [
                lax.ppermute(tail, axis, [(i, (i + 1) % count) for i in range(count)]),
                cells,
                lax.ppermute(head, axis, [((i + 1) % count, i) for i in range(count)]),
            ],
            axis=dim,
        )
    return cells


def shifted(block, axis, distance):
    devices = range(lax.axis_size(axis))
    route = [((i - distance) % len(devices), i) for i in devices]
    return lax.ppermute(block, axis, route)


def across_rows(field):
    return (field[2:] - field[:-2]) * 0.5


def along_cols(field):
    return (jnp.roll(field, -1, -1) - jnp.roll(field, 1, -1)) * 0.5


def advance(padded, coefficients, courant):
    height = padded[0]
    eastward = padded[1]
    northward = padded[2]
    new_height = height[1:-1] - courant * coefficients[0, 1:-1] * (
        across_rows(eastward) + along_cols(northward)[1:-1]
    )
    retain = 1.0 - coefficients[1, 2:-2]
    east_middle = eastward[2:-2]
    north_middle = northward[2:-2]
    new_east = (
        retain * east_middle + courant * coriolis * north_middle - courant * across_rows(new_height)
    )
    new_north = (
        retain * north_middle
        - courant * coriolis * east_middle
        - courant * along_cols(new_height)[1:-1]
    )
    return jnp.stack((new_height[1:-1], new_east, new_north))


def body(cpoint_guess, tide_forcing, depth, drag):
    coefficients = with_halo(jnp.stack((depth, drag)), (("space", 1),), 4)
    narrow = coefficients[:, 2:-2]

    def one_substep(state, courant):
        padded = with_halo(state, (("space", 1),), 2)
        return advance(padded, narrow, courant)

    def fine_map(state):
        padded = with_halo(state, (("space", 1),), 4)
        middle = advance(padded, coefficients, fine_courant)
        result = advance(middle, narrow, fine_courant)
        return result

    def coarse_map(state):
        return one_substep(state, coarse_courant)

    def pass_on(state, stride, mapper):
        result = shifted(mapper(state), "tm", stride)
        return result

    start = cpoint_guess[0]
    state = start
    for moment in range(1, tide_forcing.shape[0]):
        state = fine_map(state) + tide_forcing[moment]
    right = pass_on(state, 1, fine_map) + tide_forcing[0] - start
    rights = [right]
    for level in range(1, LEVELS):
        current = rights[-1]
        rights.append(current + pass_on(current, 2 ** (level - 1), coarse_map))
    top_stride = 2 ** (LEVELS - 1)
    points = lax.axis_size("tm") // top_stride
    position = lax.axis_index("tm")
    base = rights[-1]
    anchor = position % top_stride == 0

    def sweep(counter, correction):
        arrived = pass_on(correction, top_stride, coarse_map)
        target = jnp.logical_and(anchor, position // top_stride == counter % points)
        return jnp.where(target, arrived + base, correction)

    correction = lax.fori_loop(1, points + 1, sweep, base)
    for level in range(LEVELS - 1, 0, -1):
        stride = 2 ** (level - 1)
        arrived = pass_on(correction, stride, coarse_map)
        odd_point = position % (2 * stride) == stride
        correction = jnp.where(odd_point, arrived + rights[level - 1], correction)
    state = start + correction
    states = [state]
    for moment in range(1, tide_forcing.shape[0]):
        state = fine_map(state) + tide_forcing[moment]
        states.append(state)
    return (jnp.stack(states), right[None])


def solution(mesh):
    placed = (
        P("tm", None, "space", None),
        P("tm", None, "space", None),
        P("space", None),
        P("space", None),
    )
    return jax.shard_map(
        body,
        mesh=mesh,
        in_specs=placed,
        out_specs=(P("tm", None, "space", None), P("tm", None, "space", None)),
        check_vma=False,
    )
```

profile of v0, /device:TPU:0, one launch (start us, length us, event | category | flops | bytes accessed | tf_op | source)
XLA Modules:
  0.0 237.6 jit_solution(13293874403610139586)
XLA Ops:
  1.5 3.0 %collective-permute-start.2 = (f32[2,4,1024]{2,1,0:T(4,128)S(1)}, f32[2,4,1024]{2,1,0:T(4,128)S(1)}, u32[]{:S(2)}, u32[]{:S(2)}) collective-permute-start(f32[2,4,1024]{2,1,0:T(4,128)S(1)} %get-tuple-element.151), channel_id=1, source_target_pairs={{0,1},{1,0},{2,3},{3,2},{4,5},{5,4},{6,7},{7,6},{8,9},{9,8},{10,11... | collective-permute-start | bytes 98312 | tf_op jit(solution)/shard_map/ppermute | solution.py:21
  5.5 2.0 collective-permute-start
  10.2 1.4 collective-permute-done.1
  15.4 1.5 collective-permute-start.5
  16.9 2.1 collective-permute-done.4
  21.7 1.6 collective-permute-start.6
  23.8 2.1 collective-permute-done.6
  25.8 1.5 collective-permute-done.7
  30.1 1.5 collective-permute-start.9
  31.6 2.1 collective-permute-done.8
  36.9 1.6 collective-permute-start.10
  39.0 2.2 collective-permute-done.10
  41.2 1.3 collective-permute-done.11
  46.8 2.1 collective-permute-done.12
  51.8 1.4 collective-permute-start.14
  53.9 2.1 collective-permute-done.14
  61.5 2.1 collective-permute-done.16
  65.6 7.8 %collective-permute-done.18 = f32[3,16,1024]{2,1,0:T(8,128)S(1)} collective-permute-done((f32[3,16,1024]{2,1,0:T(8,128)S(1)}, f32[3,16,1024]{2,1,0:T(8,128)S(1)}, u32[]{:S(2)}, u32[]{:S(2)}) %collective-permute-start.18) | collective-permute-done | bytes 196640 | tf_op jit(solution)/shard_map/ppermute | solution.py:33
  73.4 1.4 collective-permute-start.19
  75.5 1.8 collective-permute-done.19
  79.3 7.8 %collective-permute-done.21 = f32[3,16,1024]{2,1,0:T(8,128)S(1)} collective-permute-done((f32[3,16,1024]{2,1,0:T(8,128)S(1)}, f32[3,16,1024]{2,1,0:T(8,128)S(1)}, u32[]{:S(2)}, u32[]{:S(2)}) %collective-permute-start.21) | collective-permute-done | bytes 196640 | tf_op jit(solution)/shard_map/ppermute | solution.py:33
  89.2 1.8 collective-permute-done.22
  92.4 8.4 %collective-permute-done.24 = f32[3,16,1024]{2,1,0:T(8,128)S(1)} collective-permute-done((f32[3,16,1024]{2,1,0:T(8,128)S(1)}, f32[3,16,1024]{2,1,0:T(8,128)S(1)}, u32[]{:S(2)}, u32[]{:S(2)}) %collective-permute-start.24) | collective-permute-done | bytes 196640 | tf_op jit(solution)/shard_map/ppermute | solution.py:33
  100.8 1.9 collective-permute-start.25
  102.9 1.8 collective-permute-done.25
  104.7 1.9 collective-permute-done.26
  107.2 7.6 %collective-permute-done.27 = f32[3,16,1024]{2,1,0:T(8,128)S(1)} collective-permute-done((f32[3,16,1024]{2,1,0:T(8,128)S(1)}, f32[3,16,1024]{2,1,0:T(8,128)S(1)}, u32[]{:S(2)}, u32[]{:S(2)}) %collective-permute-start.27) | collective-permute-done | bytes 196640 | tf_op jit(solution)/shard_map/ppermute | solution.py:33
  115.2 1.7 collective-permute-start.29
  116.9 2.0 collective-permute-done.28
  119.9 11.5 %collective-permute-done.30 = f32[3,16,1024]{2,1,0:T(8,128)S(1)} collective-permute-done((f32[3,16,1024]{2,1,0:T(8,128)S(1)}, f32[3,16,1024]{2,1,0:T(8,128)S(1)}, u32[]{:S(2)}, u32[]{:S(2)}) %collective-permute-start.30) | collective-permute-done | bytes 196640 | tf_op jit(solution)/shard_map/ppermute | solution.py:33
  131.4 2.1 collective-permute-start.31
  133.6 1.7 collective-permute-done.31
  135.4 2.0 collective-permute-done.32
  138.4 1.8 collective-permute-start.35
  140.2 1.8 collective-permute-done.34
  142.9 6.6 %collective-permute-done.36 = f32[3,16,1024]{2,1,0:T(8,128)S(1)} collective-permute-done((f32[3,16,1024]{2,1,0:T(8,128)S(1)}, f32[3,16,1024]{2,1,0:T(8,128)S(1)}, u32[]{:S(2)}, u32[]{:S(2)}) %collective-permute-start.36) | collective-permute-done | bytes 196640 | tf_op jit(solution)/shard_map/ppermute | solution.py:33
  149.6 1.8 collective-permute-start.37
  151.6 1.8 collective-permute-done.37
  153.4 1.8 collective-permute-done.38
  156.1 7.4 %collective-permute-done.39 = f32[3,16,1024]{2,1,0:T(8,128)S(1)} collective-permute-done((f32[3,16,1024]{2,1,0:T(8,128)S(1)}, f32[3,16,1024]{2,1,0:T(8,128)S(1)}, u32[]{:S(2)}, u32[]{:S(2)}) %collective-permute-start.39) | collective-permute-done | bytes 196640 | tf_op jit(solution)/shard_map/ppermute | solution.py:33
  163.9 1.8 collective-permute-start.41
  165.7 1.8 collective-permute-done.40
  168.4 8.3 %collective-permute-done.42 = f32[3,16,1024]{2,1,0:T(8,128)S(1)} collective-permute-done((f32[3,16,1024]{2,1,0:T(8,128)S(1)}, f32[3,16,1024]{2,1,0:T(8,128)S(1)}, u32[]{:S(2)}, u32[]{:S(2)}) %collective-permute-start.42) | collective-permute-done | bytes 196640 | tf_op jit(solution)/shard_map/ppermute | solution.py:33
  176.8 1.8 collective-permute-start.43
  178.9 1.8 collective-permute-done.43
  180.7 1.8 collective-permute-done.44
  183.1 7.8 %collective-permute-done.45 = f32[3,16,1024]{2,1,0:T(8,128)S(1)} collective-permute-done((f32[3,16,1024]{2,1,0:T(8,128)S(1)}, f32[3,16,1024]{2,1,0:T(8,128)S(1)}, u32[]{:S(2)}, u32[]{:S(2)}) %collective-permute-start.45) | collective-permute-done | bytes 196640 | tf_op jit(solution)/shard_map/ppermute | solution.py:33
  191.3 1.8 collective-permute-start.47
  193.1 2.1 collective-permute-done.46
  196.9 1.6 collective-permute-start.48
  199.0 2.0 collective-permute-done.48
  201.1 1.7 collective-permute-done.49
  204.4 1.7 collective-permute-start.51
  206.1 2.6 %collective-permute-done.50 = f32[3,4,1024]{2,1,0:T(4,128)S(1)} collective-permute-done((f32[3,4,1024]{2,1,0:T(4,128)S(1)}, f32[3,4,1024]{2,1,0:T(4,128)S(1)}, u32[]{:S(2)}, u32[]{:S(2)}) %collective-permute-start.50) | collective-permute-done | bytes 49184 | tf_op jit(solution)/shard_map/ppermute | solution.py:21
  211.6 1.3 collective-permute-start.53
  213.0 2.1 collective-permute-done.52
  216.9 1.4 collective-permute-start.54
  219.1 2.0 collective-permute-done.54
  221.1 1.3 collective-permute-done.55
  224.4 1.3 collective-permute-start.57
  225.8 2.0 collective-permute-done.56
  229.8 1.4 collective-permute-start.58
  231.9 2.0 collective-permute-done.58
  233.9 1.3 collective-permute-done.59
  (405 shorter events, 62.8 us)
Async XLA Ops:
  1.5 6.2 %collective-permute-start.2 = (f32[2,4,1024]{2,1,0:T(4,128)S(1)}, f32[2,4,1024]{2,1,0:T(4,128)S(1)}, u32[]{:S(2)}, u32[]{:S(2)}) collective-permute-start(f32[2,4,1024]{2,1,0:T(4,128)S(1)} %get-tuple-element.151), channel_id=1, source_target_pairs={{0,1},{1,0},{2,3},{3,2},{4,5},{5,4},{6,7},{7,6},{8,9},{9,8},{10,11... | collective-permute-start | bytes 98312 | tf_op jit(solution)/shard_map/ppermute | solution.py:21
  4.5 4.1 %collective-permute-start.3 = (f32[2,4,1024]{2,1,0:T(4,128)S(1)}, f32[2,4,1024]{2,1,0:T(4,128)S(1)}, u32[]{:S(2)}, u32[]{:S(2)}) collective-permute-start(f32[2,4,1024]{2,1,0:T(4,128)S(1)} %get-tuple-element.152), channel_id=1, source_target_pairs={{1,0},{0,1},{3,2},{2,3},{5,4},{4,5},{7,6},{6,7},{9,8},{8,9},{11,10... | collective-permute-start | bytes 98312 | tf_op jit(solution)/shard_map/ppermute | solution.py:23
  5.5 4.7 %collective-permute-start = (f32[3,4,1024]{2,1,0:T(4,128)S(1)}, f32[3,4,1024]{2,1,0:T(4,128)S(1)}, u32[]{:S(2)}, u32[]{:S(2)}) collective-permute-start(f32[3,4,1024]{2,1,0:T(4,128)S(1)} %get-tuple-element.149), channel_id=1, source_target_pairs={{0,1},{1,0},{2,3},{3,2},{4,5},{5,4},{6,7},{7,6},{8,9},{9,8},{10,11... | collective-permute-start | bytes 147464 | tf_op jit(solution)/shard_map/ppermute | solution.py:21
  7.5 4.1 %collective-permute-start.1 = (f32[3,4,1024]{2,1,0:T(4,128)S(1)}, f32[3,4,1024]{2,1,0:T(4,128)S(1)}, u32[]{:S(2)}, u32[]{:S(2)}) collective-permute-start(f32[3,4,1024]{2,1,0:T(4,128)S(1)} %get-tuple-element.150), channel_id=1, source_target_pairs={{1,0},{0,1},{3,2},{2,3},{5,4},{4,5},{7,6},{6,7},{9,8},{8,9},{11,10... | collective-permute-start | bytes 147464 | tf_op jit(solution)/shard_map/ppermute | solution.py:23
  14.8 4.2 %collective-permute-start.4 = (f32[3,4,1024]{2,1,0:T(4,128)S(1)}, f32[3,4,1024]{2,1,0:T(4,128)S(1)}, u32[]{:S(2)}, u32[]{:S(2)}) collective-permute-start(f32[3,4,1024]{2,1,0:T(4,128)S(1)} %get-tuple-element.147), channel_id=1, source_target_pairs={{0,1},{1,0},{2,3},{3,2},{4,5},{5,4},{6,7},{7,6},{8,9},{9,8},{10,11... | collective-permute-start | bytes 147464 | tf_op jit(solution)/shard_map/ppermute | solution.py:21
  15.4 4.1 %collective-permute-start.5 = (f32[3,4,1024]{2,1,0:T(4,128)S(1)}, f32[3,4,1024]{2,1,0:T(4,128)S(1)}, u32[]{:S(2)}, u32[]{:S(2)}) collective-permute-start(f32[3,4,1024]{2,1,0:T(4,128)S(1)} %get-tuple-element.148), channel_id=1, source_target_pairs={{1,0},{0,1},{3,2},{2,3},{5,4},{4,5},{7,6},{6,7},{9,8},{8,9},{11,10... | collective-permute-start | bytes 147464 | tf_op jit(solution)/shard_map/ppermute | solution.py:23
  21.7 4.2 %collective-permute-start.6 = (f32[3,4,1024]{2,1,0:T(4,128)S(1)}, f32[3,4,1024]{2,1,0:T(4,128)S(1)}, u32[]{:S(2)}, u32[]{:S(2)}) collective-permute-start(f32[3,4,1024]{2,1,0:T(4,128)S(1)} %get-tuple-element.145), channel_id=1, source_target_pairs={{0,1},{1,0},{2,3},{3,2},{4,5},{5,4},{6,7},{7,6},{8,9},{9,8},{10,11... | collective-permute-start | bytes 147464 | tf_op jit(solution)/shard_map/ppermute | solution.py:21
  23.3 4.1 %collective-permute-start.7 = (f32[3,4,1024]{2,1,0:T(4,128)S(1)}, f32[3,4,1024]{2,1,0:T(4,128)S(1)}, u32[]{:S(2)}, u32[]{:S(2)}) collective-permute-start(f32[3,4,1024]{2,1,0:T(4,128)S(1)} %get-tuple-element.146), channel_id=1, source_target_pairs={{1,0},{0,1},{3,2},{2,3},{5,4},{4,5},{7,6},{6,7},{9,8},{8,9},{11,10... | collective-permute-start | bytes 147464 | tf_op jit(solution)/shard_map/ppermute | solution.py:23
  29.5 4.2 %collective-permute-start.8 = (f32[3,4,1024]{2,1,0:T(4,128)S(1)}, f32[3,4,1024]{2,1,0:T(4,128)S(1)}, u32[]{:S(2)}, u32[]{:S(2)}) collective-permute-start(f32[3,4,1024]{2,1,0:T(4,128)S(1)} %get-tuple-element.143), channel_id=1, source_target_pairs={{0,1},{1,0},{2,3},{3,2},{4,5},{5,4},{6,7},{7,6},{8,9},{9,8},{10,11... | collective-permute-start | bytes 147464 | tf_op jit(solution)/shard_map/ppermute | solution.py:21
  30.1 4.6 %collective-permute-start.9 = (f32[3,4,1024]{2,1,0:T(4,128)S(1)}, f32[3,4,1024]{2,1,0:T(4,128)S(1)}, u32[]{:S(2)}, u32[]{:S(2)}) collective-permute-start(f32[3,4,1024]{2,1,0:T(4,128)S(1)} %get-tuple-element.144), channel_id=1, source_target_pairs={{1,0},{0,1},{3,2},{2,3},{5,4},{4,5},{7,6},{6,7},{9,8},{8,9},{11,10... | collective-permute-start | bytes 147464 | tf_op jit(solution)/shard_map/ppermute | solution.py:23
  36.9 4.3 %collective-permute-start.10 = (f32[3,4,1024]{2,1,0:T(4,128)S(1)}, f32[3,4,1024]{2,1,0:T(4,128)S(1)}, u32[]{:S(2)}, u32[]{:S(2)}) collective-permute-start(f32[3,4,1024]{2,1,0:T(4,128)S(1)} %get-tuple-element.141), channel_id=1, source_target_pairs={{0,1},{1,0},{2,3},{3,2},{4,5},{5,4},{6,7},{7,6},{8,9},{9,8},{10,11... | collective-permute-start | bytes 147464 | tf_op jit(solution)/shard_map/ppermute | solution.py:21
  38.5 4.1 %collective-permute-start.11 = (f32[3,4,1024]{2,1,0:T(4,128)S(1)}, f32[3,4,1024]{2,1,0:T(4,128)S(1)}, u32[]{:S(2)}, u32[]{:S(2)}) collective-permute-start(f32[3,4,1024]{2,1,0:T(4,128)S(1)} %get-tuple-element.142), channel_id=1, source_target_pairs={{1,0},{0,1},{3,2},{2,3},{5,4},{4,5},{7,6},{6,7},{9,8},{8,9},{11,10... | collective-permute-start | bytes 147464 | tf_op jit(solution)/shard_map/ppermute | solution.py:23
  44.7 4.2 %collective-permute-start.12 = (f32[3,4,1024]{2,1,0:T(4,128)S(1)}, f32[3,4,1024]{2,1,0:T(4,128)S(1)}, u32[]{:S(2)}, u32[]{:S(2)}) collective-permute-start(f32[3,4,1024]{2,1,0:T(4,128)S(1)} %get-tuple-element.139), channel_id=1, source_target_pairs={{0,1},{1,0},{2,3},{3,2},{4,5},{5,4},{6,7},{7,6},{8,9},{9,8},{10,11... | collective-permute-start | bytes 147464 | tf_op jit(solution)/shard_map/ppermute | solution.py:21
  45.5 4.1 %collective-permute-start.13 = (f32[3,4,1024]{2,1,0:T(4,128)S(1)}, f32[3,4,1024]{2,1,0:T(4,128)S(1)}, u32[]{:S(2)}, u32[]{:S(2)}) collective-permute-start(f32[3,4,1024]{2,1,0:T(4,128)S(1)} %get-tuple-element.140), channel_id=1, source_target_pairs={{1,0},{0,1},{3,2},{2,3},{5,4},{4,5},{7,6},{6,7},{9,8},{8,9},{11,10... | collective-permute-start | bytes 147464 | tf_op jit(solution)/shard_map/ppermute | solution.py:23
  51.8 4.2 %collective-permute-start.14 = (f32[3,4,1024]{2,1,0:T(4,128)S(1)}, f32[3,4,1024]{2,1,0:T(4,128)S(1)}, u32[]{:S(2)}, u32[]{:S(2)}) collective-permute-start(f32[3,4,1024]{2,1,0:T(4,128)S(1)} %get-tuple-element.137), channel_id=1, source_target_pairs={{0,1},{1,0},{2,3},{3,2},{4,5},{5,4},{6,7},{7,6},{8,9},{9,8},{10,11... | collective-permute-start | bytes 147464 | tf_op jit(solution)/shard_map/ppermute | solution.py:21
  53.1 4.1 %collective-permute-start.15 = (f32[3,4,1024]{2,1,0:T(4,128)S(1)}, f32[3,4,1024]{2,1,0:T(4,128)S(1)}, u32[]{:S(2)}, u32[]{:S(2)}) collective-permute-start(f32[3,4,1024]{2,1,0:T(4,128)S(1)} %get-tuple-element.138), channel_id=1, source_target_pairs={{1,0},{0,1},{3,2},{2,3},{5,4},{4,5},{7,6},{6,7},{9,8},{8,9},{11,10... | collective-permute-start | bytes 147464 | tf_op jit(solution)/shard_map/ppermute | solution.py:23
  59.4 4.2 %collective-permute-start.16 = (f32[3,4,1024]{2,1,0:T(4,128)S(1)}, f32[3,4,1024]{2,1,0:T(4,128)S(1)}, u32[]{:S(2)}, u32[]{:S(2)}) collective-permute-start(f32[3,4,1024]{2,1,0:T(4,128)S(1)} %get-tuple-element.135), channel_id=1, source_target_pairs={{0,1},{1,0},{2,3},{3,2},{4,5},{5,4},{6,7},{7,6},{8,9},{9,8},{10,11... | collective-permute-start | bytes 147464 | tf_op jit(solution)/shard_map/ppermute | solution.py:21
  60.2 4.1 %collective-permute-start.17 = (f32[3,4,1024]{2,1,0:T(4,128)S(1)}, f32[3,4,1024]{2,1,0:T(4,128)S(1)}, u32[]{:S(2)}, u32[]{:S(2)}) collective-permute-start(f32[3,4,1024]{2,1,0:T(4,128)S(1)} %get-tuple-element.136), channel_id=1, source_target_pairs={{1,0},{0,1},{3,2},{2,3},{5,4},{4,5},{7,6},{6,7},{9,8},{8,9},{11,10... | collective-permute-start | bytes 147464 | tf_op jit(solution)/shard_map/ppermute | solution.py:23
  64.9 8.5 %copy-start.1 = (f32[8,3,16,1024]{3,2,1,0:T(8,128)S(1)}, f32[8,3,16,1024]{3,2,1,0:T(8,128)}, u32[]{:S(2)}) copy-start(f32[8,3,16,1024]{3,2,1,0:T(8,128)} %param.5) | copy-start | bytes 4718596
  64.9 8.4 %copy-start.3 = (f32[1,3,16,1024]{3,2,1,0:T(8,128)S(1)}, f32[1,3,16,1024]{3,2,1,0:T(8,128)}, u32[]{:S(2)}) copy-start(f32[1,3,16,1024]{3,2,1,0:T(8,128)} %param.4) | copy-start | bytes 589828
  65.5 7.8 %collective-permute-start.18 = (f32[3,16,1024]{2,1,0:T(8,128)S(1)}, f32[3,16,1024]{2,1,0:T(8,128)S(1)}, u32[]{:S(2)}, u32[]{:S(2)}) collective-permute-start(f32[3,16,1024]{2,1,0:T(8,128)S(1)} %pad_maximum_fusion.16), channel_id=1, source_target_pairs={{30,0},{0,2},{2,4},{4,6},{6,8},{8,10},{10,12},{12,14},{14,16},{16,... | collective-permute-start | bytes 589832 | tf_op jit(solution)/shard_map/ppermute | solution.py:33
  73.4 117.5 %copy-start.2 = (f32[3,16,1024]{2,1,0:T(8,128)}, f32[3,16,1024]{2,1,0:T(8,128)S(1)}, u32[]{:S(2)}) copy-start(f32[3,16,1024]{2,1,0:T(8,128)S(1)} %fusion.7) | copy-start | bytes 589828
  73.4 3.9 %collective-permute-start.19 = (f32[3,2,1024]{2,1,0:T(2,128)S(1)}, f32[3,2,1024]{2,1,0:T(2,128)S(1)}, u32[]{:S(2)}, u32[]{:S(2)}) collective-permute-start(f32[3,2,1024]{2,1,0:T(2,128)S(1)} %get-tuple-element.133), channel_id=1, source_target_pairs={{0,1},{1,0},{2,3},{3,2},{4,5},{5,4},{6,7},{7,6},{8,9},{9,8},{10,11... | collective-permute-start | bytes 73736 | tf_op jit(solution)/shard_map/ppermute | solution.py:21
  74.8 3.8 %collective-permute-start.20 = (f32[3,2,1024]{2,1,0:T(2,128)S(1)}, f32[3,2,1024]{2,1,0:T(2,128)S(1)}, u32[]{:S(2)}, u32[]{:S(2)}) collective-permute-start(f32[3,2,1024]{2,1,0:T(2,128)S(1)} %get-tuple-element.134), channel_id=1, source_target_pairs={{1,0},{0,1},{3,2},{2,3},{5,4},{4,5},{7,6},{6,7},{9,8},{8,9},{11,10... | collective-permute-start | bytes 73736 | tf_op jit(solution)/shard_map/ppermute | solution.py:23
  79.2 7.8 %collective-permute-start.21 = (f32[3,16,1024]{2,1,0:T(8,128)S(1)}, f32[3,16,1024]{2,1,0:T(8,128)S(1)}, u32[]{:S(2)}, u32[]{:S(2)}) collective-permute-start(f32[3,16,1024]{2,1,0:T(8,128)S(1)} %pad_maximum_fusion.17), channel_id=1, source_target_pairs={{30,0},{0,2},{2,4},{4,6},{6,8},{8,10},{10,12},{12,14},{14,16},{16,... | collective-permute-start | bytes 589832 | tf_op jit(solution)/shard_map/ppermute | solution.py:33
  87.1 3.9 %collective-permute-start.22 = (f32[3,2,1024]{2,1,0:T(2,128)S(1)}, f32[3,2,1024]{2,1,0:T(2,128)S(1)}, u32[]{:S(2)}, u32[]{:S(2)}) collective-permute-start(f32[3,2,1024]{2,1,0:T(2,128)S(1)} %get-tuple-element.131), channel_id=1, source_target_pairs={{0,1},{1,0},{2,3},{3,2},{4,5},{5,4},{6,7},{7,6},{8,9},{9,8},{10,11... | collective-permute-start | bytes 73736 | tf_op jit(solution)/shard_map/ppermute | solution.py:21
  87.9 3.8 %collective-permute-start.23 = (f32[3,2,1024]{2,1,0:T(2,128)S(1)}, f32[3,2,1024]{2,1,0:T(2,128)S(1)}, u32[]{:S(2)}, u32[]{:S(2)}) collective-permute-start(f32[3,2,1024]{2,1,0:T(2,128)S(1)} %get-tuple-element.132), channel_id=1, source_target_pairs={{1,0},{0,1},{3,2},{2,3},{5,4},{4,5},{7,6},{6,7},{9,8},{8,9},{11,10... | collective-permute-start | bytes 73736 | tf_op jit(solution)/shard_map/ppermute | solution.py:23
  92.3 8.4 %collective-permute-start.24 = (f32[3,16,1024]{2,1,0:T(8,128)S(1)}, f32[3,16,1024]{2,1,0:T(8,128)S(1)}, u32[]{:S(2)}, u32[]{:S(2)}) collective-permute-start(f32[3,16,1024]{2,1,0:T(8,128)S(1)} %pad_maximum_fusion.18), channel_id=1, source_target_pairs={{28,0},{30,2},{0,4},{2,6},{4,8},{6,10},{8,12},{10,14},{12,16},{14,... | collective-permute-start | bytes 589832 | tf_op jit(solution)/shard_map/ppermute | solution.py:33
  100.8 3.9 %collective-permute-start.25 = (f32[3,2,1024]{2,1,0:T(2,128)S(1)}, f32[3,2,1024]{2,1,0:T(2,128)S(1)}, u32[]{:S(2)}, u32[]{:S(2)}) collective-permute-start(f32[3,2,1024]{2,1,0:T(2,128)S(1)} %get-tuple-element.129), channel_id=1, source_target_pairs={{0,1},{1,0},{2,3},{3,2},{4,5},{5,4},{6,7},{7,6},{8,9},{9,8},{10,11... | collective-permute-start | bytes 73736 | tf_op jit(solution)/shard_map/ppermute | solution.py:21
  102.7 3.8 %collective-permute-start.26 = (f32[3,2,1024]{2,1,0:T(2,128)S(1)}, f32[3,2,1024]{2,1,0:T(2,128)S(1)}, u32[]{:S(2)}, u32[]{:S(2)}) collective-permute-start(f32[3,2,1024]{2,1,0:T(2,128)S(1)} %get-tuple-element.130), channel_id=1, source_target_pairs={{1,0},{0,1},{3,2},{2,3},{5,4},{4,5},{7,6},{6,7},{9,8},{8,9},{11,10... | collective-permute-start | bytes 73736 | tf_op jit(solution)/shard_map/ppermute | solution.py:23
  107.2 7.6 %collective-permute-start.27 = (f32[3,16,1024]{2,1,0:T(8,128)S(1)}, f32[3,16,1024]{2,1,0:T(8,128)S(1)}, u32[]{:S(2)}, u32[]{:S(2)}) collective-permute-start(f32[3,16,1024]{2,1,0:T(8,128)S(1)} %pad_maximum_fusion.19), channel_id=1, source_target_pairs={{24,0},{26,2},{28,4},{30,6},{0,8},{2,10},{4,12},{6,14},{8,16},{10,... | collective-permute-start | bytes 589832 | tf_op jit(solution)/shard_map/ppermute | solution.py:33
  114.8 4.1 %collective-permute-start.28 = (f32[3,2,1024]{2,1,0:T(2,128)S(1)}, f32[3,2,1024]{2,1,0:T(2,128)S(1)}, u32[]{:S(2)}, u32[]{:S(2)}) collective-permute-start(f32[3,2,1024]{2,1,0:T(2,128)S(1)} %get-tuple-element.127), channel_id=1, source_target_pairs={{0,1},{1,0},{2,3},{3,2},{4,5},{5,4},{6,7},{7,6},{8,9},{9,8},{10,11... | collective-permute-start | bytes 73736 | tf_op jit(solution)/shard_map/ppermute | solution.py:21
  115.2 4.0 %collective-permute-start.29 = (f32[3,2,1024]{2,1,0:T(2,128)S(1)}, f32[3,2,1024]{2,1,0:T(2,128)S(1)}, u32[]{:S(2)}, u32[]{:S(2)}) collective-permute-start(f32[3,2,1024]{2,1,0:T(2,128)S(1)} %get-tuple-element.128), channel_id=1, source_target_pairs={{1,0},{0,1},{3,2},{2,3},{5,4},{4,5},{7,6},{6,7},{9,8},{8,9},{11,10... | collective-permute-start | bytes 73736 | tf_op jit(solution)/shard_map/ppermute | solution.py:23
  119.8 11.5 %collective-permute-start.30 = (f32[3,16,1024]{2,1,0:T(8,128)S(1)}, f32[3,16,1024]{2,1,0:T(8,128)S(1)}, u32[]{:S(2)}, u32[]{:S(2)}) collective-permute-start(f32[3,16,1024]{2,1,0:T(8,128)S(1)} %pad_maximum_fusion.20), channel_id=1, source_target_pairs={{16,0},{18,2},{20,4},{22,6},{24,8},{26,10},{28,12},{30,14},{0,16},... | collective-permute-start | bytes 589832 | tf_op jit(solution)/shard_map/ppermute | solution.py:33
  131.4 3.9 %collective-permute-start.31 = (f32[3,2,1024]{2,1,0:T(2,128)S(1)}, f32[3,2,1024]{2,1,0:T(2,128)S(1)}, u32[]{:S(2)}, u32[]{:S(2)}) collective-permute-start(f32[3,2,1024]{2,1,0:T(2,128)S(1)} %get-tuple-element.125), channel_id=1, source_target_pairs={{0,1},{1,0},{2,3},{3,2},{4,5},{5,4},{6,7},{7,6},{8,9},{9,8},{10,11... | collective-permute-start | bytes 73736 | tf_op jit(solution)/shard_map/while/body/eval_jaxpr/ppermute | solution.py:21
  133.6 3.8 %collective-permute-start.32 = (f32[3,2,1024]{2,1,0:T(2,128)S(1)}, f32[3,2,1024]{2,1,0:T(2,128)S(1)}, u32[]{:S(2)}, u32[]{:S(2)}) collective-permute-start(f32[3,2,1024]{2,1,0:T(2,128)S(1)} %get-tuple-element.126), channel_id=1, source_target_pairs={{1,0},{0,1},{3,2},{2,3},{5,4},{4,5},{7,6},{6,7},{9,8},{8,9},{11,10... | collective-permute-start | bytes 73736 | tf_op jit(solution)/shard_map/while/body/eval_jaxpr/ppermute | solution.py:23
  138.0 0.1 collective-permute-start.33
  138.1 3.9 %collective-permute-start.34 = (f32[3,2,1024]{2,1,0:T(2,128)S(1)}, f32[3,2,1024]{2,1,0:T(2,128)S(1)}, u32[]{:S(2)}, u32[]{:S(2)}) collective-permute-start(f32[3,2,1024]{2,1,0:T(2,128)S(1)} %get-tuple-element.123), channel_id=1, source_target_pairs={{0,1},{1,0},{2,3},{3,2},{4,5},{5,4},{6,7},{7,6},{8,9},{9,8},{10,11... | collective-permute-start | bytes 73736 | tf_op jit(solution)/shard_map/ppermute | solution.py:21
  138.4 3.8 %collective-permute-start.35 = (f32[3,2,1024]{2,1,0:T(2,128)S(1)}, f32[3,2,1024]{2,1,0:T(2,128)S(1)}, u32[]{:S(2)}, u32[]{:S(2)}) collective-permute-start(f32[3,2,1024]{2,1,0:T(2,128)S(1)} %get-tuple-element.124), channel_id=1, source_target_pairs={{1,0},{0,1},{3,2},{2,3},{5,4},{4,5},{7,6},{6,7},{9,8},{8,9},{11,10... | collective-permute-start | bytes 73736 | tf_op jit(solution)/shard_map/ppermute | solution.py:23
  142.9 6.6 %collective-permute-start.36 = (f32[3,16,1024]{2,1,0:T(8,128)S(1)}, f32[3,16,1024]{2,1,0:T(8,128)S(1)}, u32[]{:S(2)}, u32[]{:S(2)}) collective-permute-start(f32[3,16,1024]{2,1,0:T(8,128)S(1)} %pad_maximum_fusion.22), channel_id=1, source_target_pairs={{16,0},{18,2},{20,4},{22,6},{24,8},{26,10},{28,12},{30,14},{0,16},... | collective-permute-start | bytes 589832 | tf_op jit(solution)/shard_map/ppermute | solution.py:33
  149.6 3.9 %collective-permute-start.37 = (f32[3,2,1024]{2,1,0:T(2,128)S(1)}, f32[3,2,1024]{2,1,0:T(2,128)S(1)}, u32[]{:S(2)}, u32[]{:S(2)}) collective-permute-start(f32[3,2,1024]{2,1,0:T(2,128)S(1)} %get-tuple-element.121), channel_id=1, source_target_pairs={{0,1},{1,0},{2,3},{3,2},{4,5},{5,4},{6,7},{7,6},{8,9},{9,8},{10,11... | collective-permute-start | bytes 73736 | tf_op jit(solution)/shard_map/ppermute | solution.py:21
  151.4 3.8 %collective-permute-start.38 = (f32[3,2,1024]{2,1,0:T(2,128)S(1)}, f32[3,2,1024]{2,1,0:T(2,128)S(1)}, u32[]{:S(2)}, u32[]{:S(2)}) collective-permute-start(f32[3,2,1024]{2,1,0:T(2,128)S(1)} %get-tuple-element.122), channel_id=1, source_target_pairs={{1,0},{0,1},{3,2},{2,3},{5,4},{4,5},{7,6},{6,7},{9,8},{8,9},{11,10... | collective-permute-start | bytes 73736 | tf_op jit(solution)/shard_map/ppermute | solution.py:23
  155.8 7.7 %collective-permute-start.39 = (f32[3,16,1024]{2,1,0:T(8,128)S(1)}, f32[3,16,1024]{2,1,0:T(8,128)S(1)}, u32[]{:S(2)}, u32[]{:S(2)}) collective-permute-start(f32[3,16,1024]{2,1,0:T(8,128)S(1)} %pad_maximum_fusion.23), channel_id=1, source_target_pairs={{24,0},{26,2},{28,4},{30,6},{0,8},{2,10},{4,12},{6,14},{8,16},{10,... | collective-permute-start | bytes 589832 | tf_op jit(solution)/shard_map/ppermute | solution.py:33
  163.6 3.9 %collective-permute-start.40 = (f32[3,2,1024]{2,1,0:T(2,128)S(1)}, f32[3,2,1024]{2,1,0:T(2,128)S(1)}, u32[]{:S(2)}, u32[]{:S(2)}) collective-permute-start(f32[3,2,1024]{2,1,0:T(2,128)S(1)} %get-tuple-element.119), channel_id=1, source_target_pairs={{0,1},{1,0},{2,3},{3,2},{4,5},{5,4},{6,7},{7,6},{8,9},{9,8},{10,11... | collective-permute-start | bytes 73736 | tf_op jit(solution)/shard_map/ppermute | solution.py:21
  163.9 3.8 %collective-permute-start.41 = (f32[3,2,1024]{2,1,0:T(2,128)S(1)}, f32[3,2,1024]{2,1,0:T(2,128)S(1)}, u32[]{:S(2)}, u32[]{:S(2)}) collective-permute-start(f32[3,2,1024]{2,1,0:T(2,128)S(1)} %get-tuple-element.120), channel_id=1, source_target_pairs={{1,0},{0,1},{3,2},{2,3},{5,4},{4,5},{7,6},{6,7},{9,8},{8,9},{11,10... | collective-permute-start | bytes 73736 | tf_op jit(solution)/shard_map/ppermute | solution.py:23
  168.3 8.4 %collective-permute-start.42 = (f32[3,16,1024]{2,1,0:T(8,128)S(1)}, f32[3,16,1024]{2,1,0:T(8,128)S(1)}, u32[]{:S(2)}, u32[]{:S(2)}) collective-permute-start(f32[3,16,1024]{2,1,0:T(8,128)S(1)} %pad_maximum_fusion.24), channel_id=1, source_target_pairs={{28,0},{30,2},{0,4},{2,6},{4,8},{6,10},{8,12},{10,14},{12,16},{14,... | collective-permute-start | bytes 589832 | tf_op jit(solution)/shard_map/ppermute | solution.py:33
  176.8 3.9 %collective-permute-start.43 = (f32[3,2,1024]{2,1,0:T(2,128)S(1)}, f32[3,2,1024]{2,1,0:T(2,128)S(1)}, u32[]{:S(2)}, u32[]{:S(2)}) collective-permute-start(f32[3,2,1024]{2,1,0:T(2,128)S(1)} %get-tuple-element.117), channel_id=1, source_target_pairs={{0,1},{1,0},{2,3},{3,2},{4,5},{5,4},{6,7},{7,6},{8,9},{9,8},{10,11... | collective-permute-start | bytes 73736 | tf_op jit(solution)/shard_map/ppermute | solution.py:21
  178.6 3.8 %collective-permute-start.44 = (f32[3,2,1024]{2,1,0:T(2,128)S(1)}, f32[3,2,1024]{2,1,0:T(2,128)S(1)}, u32[]{:S(2)}, u32[]{:S(2)}) collective-permute-start(f32[3,2,1024]{2,1,0:T(2,128)S(1)} %get-tuple-element.118), channel_id=1, source_target_pairs={{1,0},{0,1},{3,2},{2,3},{5,4},{4,5},{7,6},{6,7},{9,8},{8,9},{11,10... | collective-permute-start | bytes 73736 | tf_op jit(solution)/shard_map/ppermute | solution.py:23
  183.0 7.8 %collective-permute-start.45 = (f32[3,16,1024]{2,1,0:T(8,128)S(1)}, f32[3,16,1024]{2,1,0:T(8,128)S(1)}, u32[]{:S(2)}, u32[]{:S(2)}) collective-permute-start(f32[3,16,1024]{2,1,0:T(8,128)S(1)} %pad_maximum_fusion.25), channel_id=1, source_target_pairs={{30,0},{0,2},{2,4},{4,6},{6,8},{8,10},{10,12},{12,14},{14,16},{16,... | collective-permute-start | bytes 589832 | tf_op jit(solution)/shard_map/ppermute | solution.py:33
  191.0 4.2 %collective-permute-start.46 = (f32[3,4,1024]{2,1,0:T(4,128)S(1)}, f32[3,4,1024]{2,1,0:T(4,128)S(1)}, u32[]{:S(2)}, u32[]{:S(2)}) collective-permute-start(f32[3,4,1024]{2,1,0:T(4,128)S(1)} %get-tuple-element.115), channel_id=1, source_target_pairs={{0,1},{1,0},{2,3},{3,2},{4,5},{5,4},{6,7},{7,6},{8,9},{9,8},{10,11... | collective-permute-start | bytes 147464 | tf_op jit(solution)/shard_map/ppermute | solution.py:21
  191.3 4.4 %collective-permute-start.47 = (f32[3,4,1024]{2,1,0:T(4,128)S(1)}, f32[3,4,1024]{2,1,0:T(4,128)S(1)}, u32[]{:S(2)}, u32[]{:S(2)}) collective-permute-start(f32[3,4,1024]{2,1,0:T(4,128)S(1)} %get-tuple-element.116), channel_id=1, source_target_pairs={{1,0},{0,1},{3,2},{2,3},{5,4},{4,5},{7,6},{6,7},{9,8},{8,9},{11,10... | collective-permute-start | bytes 147464 | tf_op jit(solution)/shard_map/ppermute | solution.py:23
  196.9 4.2 %collective-permute-start.48 = (f32[3,4,1024]{2,1,0:T(4,128)S(1)}, f32[3,4,1024]{2,1,0:T(4,128)S(1)}, u32[]{:S(2)}, u32[]{:S(2)}) collective-permute-start(f32[3,4,1024]{2,1,0:T(4,128)S(1)} %get-tuple-element.113), channel_id=1, source_target_pairs={{0,1},{1,0},{2,3},{3,2},{4,5},{5,4},{6,7},{7,6},{8,9},{9,8},{10,11... | collective-permute-start | bytes 147464 | tf_op jit(solution)/shard_map/ppermute | solution.py:21
  198.5 4.3 %collective-permute-start.49 = (f32[3,4,1024]{2,1,0:T(4,128)S(1)}, f32[3,4,1024]{2,1,0:T(4,128)S(1)}, u32[]{:S(2)}, u32[]{:S(2)}) collective-permute-start(f32[3,4,1024]{2,1,0:T(4,128)S(1)} %get-tuple-element.114), channel_id=1, source_target_pairs={{1,0},{0,1},{3,2},{2,3},{5,4},{4,5},{7,6},{6,7},{9,8},{8,9},{11,10... | collective-permute-start | bytes 147464 | tf_op jit(solution)/shard_map/ppermute | solution.py:23
  204.0 4.7 %collective-permute-start.50 = (f32[3,4,1024]{2,1,0:T(4,128)S(1)}, f32[3,4,1024]{2,1,0:T(4,128)S(1)}, u32[]{:S(2)}, u32[]{:S(2)}) collective-permute-start(f32[3,4,1024]{2,1,0:T(4,128)S(1)} %get-tuple-element.111), channel_id=1, source_target_pairs={{0,1},{1,0},{2,3},{3,2},{4,5},{5,4},{6,7},{7,6},{8,9},{9,8},{10,11... | collective-permute-start | bytes 147464 | tf_op jit(solution)/shard_map/ppermute | solution.py:21
  204.4 5.2 %collective-permute-start.51 = (f32[3,4,1024]{2,1,0:T(4,128)S(1)}, f32[3,4,1024]{2,1,0:T(4,128)S(1)}, u32[]{:S(2)}, u32[]{:S(2)}) collective-permute-start(f32[3,4,1024]{2,1,0:T(4,128)S(1)} %get-tuple-element.112), channel_id=1, source_target_pairs={{1,0},{0,1},{3,2},{2,3},{5,4},{4,5},{7,6},{6,7},{9,8},{8,9},{11,10... | collective-permute-start | bytes 147464 | tf_op jit(solution)/shard_map/ppermute | solution.py:23
  210.9 4.2 %collective-permute-start.52 = (f32[3,4,1024]{2,1,0:T(4,128)S(1)}, f32[3,4,1024]{2,1,0:T(4,128)S(1)}, u32[]{:S(2)}, u32[]{:S(2)}) collective-permute-start(f32[3,4,1024]{2,1,0:T(4,128)S(1)} %get-tuple-element.109), channel_id=1, source_target_pairs={{0,1},{1,0},{2,3},{3,2},{4,5},{5,4},{6,7},{7,6},{8,9},{9,8},{10,11... | collective-permute-start | bytes 147464 | tf_op jit(solution)/shard_map/ppermute | solution.py:21
  211.6 4.1 %collective-permute-start.53 = (f32[3,4,1024]{2,1,0:T(4,128)S(1)}, f32[3,4,1024]{2,1,0:T(4,128)S(1)}, u32[]{:S(2)}, u32[]{:S(2)}) collective-permute-start(f32[3,4,1024]{2,1,0:T(4,128)S(1)} %get-tuple-element.110), channel_id=1, source_target_pairs={{1,0},{0,1},{3,2},{2,3},{5,4},{4,5},{7,6},{6,7},{9,8},{8,9},{11,10... | collective-permute-start | bytes 147464 | tf_op jit(solution)/shard_map/ppermute | solution.py:23
  216.9 4.2 %collective-permute-start.54 = (f32[3,4,1024]{2,1,0:T(4,128)S(1)}, f32[3,4,1024]{2,1,0:T(4,128)S(1)}, u32[]{:S(2)}, u32[]{:S(2)}) collective-permute-start(f32[3,4,1024]{2,1,0:T(4,128)S(1)} %get-tuple-element.107), channel_id=1, source_target_pairs={{0,1},{1,0},{2,3},{3,2},{4,5},{5,4},{6,7},{7,6},{8,9},{9,8},{10,11... | collective-permute-start | bytes 147464 | tf_op jit(solution)/shard_map/ppermute | solution.py:21
  218.3 4.1 %collective-permute-start.55 = (f32[3,4,1024]{2,1,0:T(4,128)S(1)}, f32[3,4,1024]{2,1,0:T(4,128)S(1)}, u32[]{:S(2)}, u32[]{:S(2)}) collective-permute-start(f32[3,4,1024]{2,1,0:T(4,128)S(1)} %get-tuple-element.108), channel_id=1, source_target_pairs={{1,0},{0,1},{3,2},{2,3},{5,4},{4,5},{7,6},{6,7},{9,8},{8,9},{11,10... | collective-permute-start | bytes 147464 | tf_op jit(solution)/shard_map/ppermute | solution.py:23
  223.7 4.2 %collective-permute-start.56 = (f32[3,4,1024]{2,1,0:T(4,128)S(1)}, f32[3,4,1024]{2,1,0:T(4,128)S(1)}, u32[]{:S(2)}, u32[]{:S(2)}) collective-permute-start(f32[3,4,1024]{2,1,0:T(4,128)S(1)} %get-tuple-element.105), channel_id=1, source_target_pairs={{0,1},{1,0},{2,3},{3,2},{4,5},{5,4},{6,7},{7,6},{8,9},{9,8},{10,11... | collective-permute-start | bytes 147464 | tf_op jit(solution)/shard_map/ppermute | solution.py:21
  224.4 4.1 %collective-permute-start.57 = (f32[3,4,1024]{2,1,0:T(4,128)S(1)}, f32[3,4,1024]{2,1,0:T(4,128)S(1)}, u32[]{:S(2)}, u32[]{:S(2)}) collective-permute-start(f32[3,4,1024]{2,1,0:T(4,128)S(1)} %get-tuple-element.106), channel_id=1, source_target_pairs={{1,0},{0,1},{3,2},{2,3},{5,4},{4,5},{7,6},{6,7},{9,8},{8,9},{11,10... | collective-permute-start | bytes 147464 | tf_op jit(solution)/shard_map/ppermute | solution.py:23
  229.8 4.2 %collective-permute-start.58 = (f32[3,4,1024]{2,1,0:T(4,128)S(1)}, f32[3,4,1024]{2,1,0:T(4,128)S(1)}, u32[]{:S(2)}, u32[]{:S(2)}) collective-permute-start(f32[3,4,1024]{2,1,0:T(4,128)S(1)} %get-tuple-element.103), channel_id=1, source_target_pairs={{0,1},{1,0},{2,3},{3,2},{4,5},{5,4},{6,7},{7,6},{8,9},{9,8},{10,11... | collective-permute-start | bytes 147464 | tf_op jit(solution)/shard_map/ppermute | solution.py:21
  231.2 4.1 %collective-permute-start.59 = (f32[3,4,1024]{2,1,0:T(4,128)S(1)}, f32[3,4,1024]{2,1,0:T(4,128)S(1)}, u32[]{:S(2)}, u32[]{:S(2)}) collective-permute-start(f32[3,4,1024]{2,1,0:T(4,128)S(1)} %get-tuple-element.104), channel_id=1, source_target_pairs={{1,0},{0,1},{3,2},{2,3},{5,4},{4,5},{7,6},{6,7},{9,8},{8,9},{11,10... | collective-permute-start | bytes 147464 | tf_op jit(solution)/shard_map/ppermute | solution.py:23
  236.5 1.1 copy-start.4
  (1 other events, 0.8 us)
where the time goes:
time: 238 us
  waiting for transfers between devices  147 us (62%)
  starting transfers between devices  54.2 us (23%)
  other arithmetic  19.4 us (8%)
  local copies, waits for them, and re-layouts  15 us (6%)
  between operations  2.6 us (1%)
    ppermute x10, waiting for transfers between devices, shifted(): return lax.ppermute(block, axis, route)  73 us
    ppermute x25, waiting for transfers between devices, with_halo(): lax.ppermute(tail, axis, [(i, (i + 1) % count) for i in range(count)])  46.5 us
    ppermute x25, starting transfers between devices, with_halo(): lax.ppermute(tail, axis, [(i, (i + 1) % count) for i in range(count)])  29.8 us
    ppermute x25, waiting for transfers between devices, with_halo(): lax.ppermute(head, axis, [((i + 1) % count, i) for i in range(count)])  27.1 us
    ppermute x25, starting transfers between devices, with_halo(): lax.ppermute(head, axis, [((i + 1) % count, i) for i in range(count)])  23.6 us
    slice x156, local copies, waits for them, and re-layouts, along_cols(): return (jnp.roll(field, -1, -1) - jnp.roll(field, 1, -1)) * 0.5  12.2 us
    add x13, other arithmetic, body(): state = fine_map(state) + tide_forcing[moment]  6.85 us
  transfers between devices with their start and end apart: 60, of which 58 were waited for; matrix products, arithmetic and copies ran while one was open for 1% of the time, Pallas kernels for 0%

commit v1 on v0

--- a/solution.py
+++ b/solution.py
@@ -1,6 +1,8 @@
 import jax
 import jax.numpy as jnp
 from jax import lax
+from jax.experimental import pallas as pl
+from jax.experimental.pallas import tpu as pltpu
 from jax.sharding import PartitionSpec as P
 
 LEVELS = 5
@@ -117,6 +119,367 @@
     return (jnp.stack(states), right[None])
 
 
+def cycle_kernel(
+    guess, forcing, depth, drag, out, residual,
+    coef, track, mid, edges, edges_in, ahead, ahead_in, first, second, third, fourth,
+    climb, final, final_in, residual_in, relax, wave,
+    coef_sems, edge_send, edge_recv, ahead_sems, res_send, res_recv,
+    first_sems, second_sems, third_sems, fourth_send, fourth_recv, relay_send,
+    sibling_sems, final_sems,
+):
+    tm = lax.axis_index("tm")
+    sp = lax.axis_index("space")
+    count = lax.axis_size("tm")
+    moments = forcing.shape[0]
+    own = guess.shape[2]
+    rows = 2 * own
+    cols = guess.shape[3]
+    lanes = 128
+    strips = cols // lanes
+    other = 1 - sp
+    before = (tm + count - 1) % count
+    after = (tm + 1) % count
+    odd = tm % 2
+    chip = (tm // 2) % 2
+    layer = tm // 4
+    pair = layer % 2
+    half = layer // 2
+    facing = tm + 2 - 4 * chip
+    beside = tm + 4 - 8 * pair
+    inner = pair != half
+    inward = (tm + 4 - 8 * half + count) % count
+    outward = (tm - 4 + 8 * half + count) % count
+
+    def remote(src, dst, send, recv, to):
+        return pltpu.make_async_remote_copy(
+            src_ref=src, dst_ref=dst, send_sem=send, recv_sem=recv,
+            device_id=to, device_id_type=pl.DeviceIdType.MESH,
+        )
+
+    barrier = pltpu.get_barrier_semaphore()
+    partners = [
+        (tm, other), (before, sp), (after, sp), (before, other), (after, other),
+        (facing, sp), ((tm + 4) % count, sp), ((tm + count - 4) % count, sp),
+    ]
+    for to in partners:
+        pl.semaphore_signal(barrier, inc=1, device_id=to, device_id_type=pl.DeviceIdType.MESH)
+
+    lane = lax.broadcasted_iota(jnp.int32, (rows, lanes), 1)
+    first_lane = lane == 0
+    last_lane = lane == lanes - 1
+
+    def strip(index):
+        return pl.ds(pl.multiple_of(index * lanes, lanes), lanes)
+
+    def down_rows(a):
+        return pltpu.roll(a, rows - 1, 0) - pltpu.roll(a, 1, 0)
+
+    def down_cols(a, following, preceding):
+        return pltpu.roll(jnp.where(first_lane, following, a), lanes - 1, 1) - pltpu.roll(
+            jnp.where(last_lane, preceding, a), 1, 1
+        )
+
+    def substep(src, dst, courant):
+        def heights(j, carry):
+            here = strip(j)
+            u = src[1, :, here]
+            v = src[2, :, here]
+            spread = down_rows(u) + down_cols(
+                v, src[2, :, strip((j + 1) % strips)], src[2, :, strip((j + strips - 1) % strips)]
+            )
+            dst[0, :, here] = src[0, :, here] - courant * coef[0, :, here] * spread
+            return carry
+
+        def speeds(j, carry):
+            here = strip(j)
+            u = src[1, :, here]
+            v = src[2, :, here]
+            h = dst[0, :, here]
+            retain = coef[1, :, here]
+            dst[1, :, here] = (
+                retain * u + courant * coriolis * v - courant * 0.5 * down_rows(h)
+            )
+            dst[2, :, here] = (
+                retain * v - courant * coriolis * u - courant * 0.5 * down_cols(
+                    h, dst[0, :, strip((j + 1) % strips)],
+                    dst[0, :, strip((j + strips - 1) % strips)],
+                )
+            )
+            return carry
+
+        lax.fori_loop(0, strips, heights, 0, unroll=True)
+        lax.fori_loop(0, strips, speeds, 0, unroll=True)
+
+    def fine(src, dst):
+        substep(src, mid, fine_courant)
+        substep(mid, dst, fine_courant)
+
+    def coarse(src, dst):
+        substep(src, dst, coarse_courant)
+
+    coef[0, 0:own] = 0.5 * depth[...]
+    coef[1, 0:own] = 1.0 - drag[...]
+    track[0, :, 0:own] = guess[0]
+    track[0, :, own:rows] = jnp.zeros((3, own, cols), jnp.float32)
+    ahead[...] = forcing[0] - guess[0]
+    relax[0, :, 0:own] = jnp.zeros((3, own, cols), jnp.float32)
+
+    pl.semaphore_wait(barrier, len(partners))
+    coef_copy = remote(
+        coef.at[:, 0:own], coef.at[:, own:rows], coef_sems.at[0], coef_sems.at[1], (tm, other)
+    )
+    coef_copy.start()
+    ahead_copy = remote(ahead, ahead_in, ahead_sems.at[0], ahead_sems.at[1], (before, sp))
+    ahead_copy.start()
+
+    def edge_copy(moment):
+        return remote(
+            edges.at[moment], edges_in.at[moment], edge_send.at[moment], edge_recv.at[moment],
+            (tm, other),
+        )
+
+    upper = lax.broadcasted_iota(jnp.int32, (3, own // 2, cols), 1) < 4
+    coef_copy.wait()
+
+    def propagate(moment, carry):
+        previous = moment - 1
+        edges[previous] = jnp.where(
+            upper, track[previous, :, 0 : own // 2], track[previous, :, own // 2 : own]
+        )
+        edge_copy(previous).start()
+        fine(track.at[previous], track.at[moment])
+        track[moment, :, 0:own] += forcing[moment]
+        return carry
+
+    lax.fori_loop(1, moments, propagate, 0)
+    mine = first.at[odd]
+    fine(track.at[moments - 1], mine)
+    ahead_copy.wait()
+    first[odd, :, 0:own] += ahead_in[...]
+
+    first_copy = remote(first.at[0], first.at[0], first_sems.at[0], first_sems.at[1], (after, sp))
+
+    @pl.when(odd == 0)
+    def _():
+        first_copy.start()
+
+    res_here = remote(
+        first.at[odd, :, 0:own], residual_in.at[0], res_send.at[0], res_recv.at[0], (after, sp)
+    )
+    res_there = remote(
+        first.at[odd, :, own:rows], residual_in.at[1], res_send.at[1], res_recv.at[1],
+        (after, other),
+    )
+
+    def relaxed(low, high):
+        def step(moment, carry):
+            previous = moment - 1
+            edge_copy(previous).wait()
+            a = previous % 2
+            b = moment % 2
+            relax[a, :, own : own + own // 2] = edges_in[previous]
+            relax[a, :, own + own // 2 : rows] = edges_in[previous]
+            fine(relax.at[a], relax.at[b])
+            track[moment, :, 0:own] += relax[b, :, 0:own]
+            return carry
+
+        lax.fori_loop(low, high, step, 0)
+
+    second_copy = remote(
+        second.at[chip], second.at[chip], second_sems.at[0], second_sems.at[1], (facing, sp)
+    )
+    second_in = remote(
+        second.at[1 - chip], second.at[1 - chip], second_sems.at[0], second_sems.at[1],
+        (facing, sp),
+    )
+    third_copy = remote(
+        third.at[pair], third.at[pair], third_sems.at[0], third_sems.at[1], (beside, sp)
+    )
+    third_in = remote(
+        third.at[1 - pair], third.at[1 - pair], third_sems.at[0], third_sems.at[1], (beside, sp)
+    )
+
+    def gather(field, to):
+        return remote(
+            fourth.at[half, field], fourth.at[half, field], fourth_send.at[field],
+            fourth_recv.at[field], (to, sp),
+        )
+
+    def relay(field, to):
+        return remote(
+            fourth.at[1 - half, field], fourth.at[1 - half, field], relay_send.at[field],
+            fourth_recv.at[field], (to, sp),
+        )
+
+    @pl.when(odd == 1)
+    def _():
+        first_copy.wait_recv()
+        coarse(first.at[0], second.at[chip])
+        second[chip] += first[1]
+        second_copy.start()
+
+    res_here.start()
+    res_there.start()
+    relaxed(1, 3)
+
+    @pl.when(odd == 1)
+    def _():
+        second_in.wait_recv()
+        coarse(second.at[0], third.at[pair])
+        third[pair] += second[1]
+        third_copy.start()
+
+    relaxed(3, 5)
+
+    @pl.when(odd == 1)
+    def _():
+        third_in.wait_recv()
+        coarse(third.at[0], fourth.at[half])
+        fourth[half] += third[1]
+
+        @pl.when(inner)
+        def _():
+            for field in range(3):
+                gather(field, inward).start()
+
+    relaxed(5, moments)
+
+    @pl.when(odd == 1)
+    def _():
+        for field in range(3):
+            relay(field, inward).wait_recv()
+
+            @pl.when(inner)
+            def _():
+                relay(field, outward).start()
+
+        coarse(fourth.at[0], climb.at[0])
+        climb[0] += fourth[1]
+        coarse(climb.at[0], climb.at[1])
+        climb[1] += climb[0]
+
+        def rise(take, src, dst, lower):
+            @pl.when(take == 1)
+            def _():
+                coarse(src, dst)
+                dst[...] += lower[...]
+
+            @pl.when(take == 0)
+            def _():
+                dst[...] = src[...]
+
+        rise(half, climb.at[1], climb.at[0], fourth.at[0])
+        rise(pair, climb.at[0], climb.at[1], third.at[0])
+        rise(chip, climb.at[1], climb.at[0], second.at[0])
+
+    sibling = remote(climb.at[0], final, sibling_sems.at[0], sibling_sems.at[1], (before, sp))
+
+    @pl.when(odd == 1)
+    def _():
+        sibling.start()
+        coarse(climb.at[0], final)
+        final[...] += first[0]
+
+    @pl.when(odd == 0)
+    def _():
+        sibling.wait_recv()
+
+    final_copy = remote(final, final_in, final_sems.at[0], final_sems.at[1], (tm, other))
+    final_copy.start()
+
+    res_here.wait()
+    res_there.wait()
+    residual[0] = residual_in[0] + residual_in[1]
+
+    @pl.when(odd == 0)
+    def _():
+        first_copy.wait_send()
+
+    @pl.when(odd == 1)
+    def _():
+        second_copy.wait_send()
+        third_copy.wait_send()
+        sibling.wait_send()
+
+        @pl.when(inner)
+        def _():
+            for field in range(3):
+                gather(field, inward).wait_send()
+                relay(field, outward).wait_send()
+
+    final_copy.wait()
+    wave[0, :, 0:own] = final[:, 0:own] + final_in[:, own:rows]
+    wave[0, :, own:rows] = final[:, own:rows] + final_in[:, 0:own]
+    out[0] = guess[0] + wave[0, :, 0:own]
+
+    def correct(moment, carry):
+        a = (moment - 1) % 2
+        b = moment % 2
+        fine(wave.at[a], wave.at[b])
+        out[moment] = track[moment, :, 0:own] + wave[b, :, 0:own]
+        return carry
+
+    lax.fori_loop(1, moments, correct, 0)
+
+
+def kernel_body(cpoint_guess, tide_forcing, depth, drag):
+    moments, fields, own, cols = tide_forcing.shape
+    block = (fields, 2 * own, cols)
+    part = (fields, own, cols)
+    edge = (moments - 1, fields, own // 2, cols)
+
+    def held(*shape):
+        return pltpu.VMEM(shape, jnp.float32)
+
+    dma = pltpu.SemaphoreType.DMA
+    vmem = pl.BlockSpec(memory_space=pltpu.VMEM)
+    return pl.pallas_call(
+        cycle_kernel,
+        out_shape=(
+            jax.ShapeDtypeStruct(tide_forcing.shape, jnp.float32),
+            jax.ShapeDtypeStruct(cpoint_guess.shape, jnp.float32),
+        ),
+        in_specs=[vmem] * 4,
+        out_specs=(vmem, vmem),
+        scratch_shapes=[
+            held(2, 2 * own, cols),
+            held(moments, *block),
+            held(*block),
+            held(*edge),
+            held(*edge),
+            held(*part),
+            held(*part),
+            held(2, *block),
+            held(2, *block),
+            held(2, *block),
+            held(2, *block),
+            held(2, *block),
+            held(*block),
+            held(*block),
+            held(2, *part),
+            held(2, *block),
+            held(2, *block),
+            dma((2,)),
+            dma((moments - 1,)),
+            dma((moments - 1,)),
+            dma((2,)),
+            dma((2,)),
+            dma((2,)),
+            dma((2,)),
+            dma((2,)),
+            dma((2,)),
+            dma((3,)),
+            dma((3,)),
+            dma((3,)),
+            dma((2,)),
+            dma((2,)),
+        ],
+        compiler_params=pltpu.CompilerParams(
+            collective_id=0, has_side_effects=True, vmem_limit_bytes=48 * 1024 * 1024
+        ),
+    )(cpoint_guess, tide_forcing, depth, drag)
+
+
 def solution(mesh):
     placed = (
         P("tm", None, "space", None),
@@ -124,8 +487,10 @@
         P("space", None),
         P("space", None),
     )
+    one_top_point = mesh.shape["tm"] == 2 ** (LEVELS - 1)
+    fits = one_top_point and mesh.shape["space"] == 2
     return jax.shard_map(
-        body,
+        kernel_body if fits else body,
         mesh=mesh,
         in_specs=placed,
         out_specs=(P("tm", None, "space", None), P("tm", None, "space", None)),

time: 238 us -> 65 us (0.27)
  waiting for transfers between devices: 147 us -> 0 us
  Pallas kernels: 0 us -> 58.2 us
  starting transfers between devices: 54.2 us -> 0 us
  other arithmetic: 19.4 us -> 0 us
  local copies, waits for them, and re-layouts: 15 us -> 5.83 us
    ppermute x60 -> x0, waiting for transfers between devices: 147 us -> none  [the longest x10 73 us: shifted(): return lax.ppermute(block, axis, route)]
    pallas_call x0 -> x1, Pallas kernels: none -> 58.2 us  [kernel_body(): pl.pallas_call(cycle_kernel, out_shape=(jax.ShapeDtypeStruct(tide_forcing...]
    ppermute x60 -> x0, starting transfers between devices: 54.2 us -> none  [the longest x25 29.8 us: with_halo(): lax.ppermute(tail, axis, [(i, (i + 1) % count) for i in range(count)])]
    slice x180 -> x0, local copies, waits for them, and re-layouts: 13.6 us -> none  [the longest x156 12.2 us: along_cols(): return (jnp.roll(field, -1, -1) - jnp.roll(field, 1, -1)) * 0.5]
    add x17 -> x0, other arithmetic: 6.94 us -> none  [the longest x13 6.85 us: body(): state = fine_map(state) + tide_forcing[moment]]
    sub x61 -> x0, other arithmetic: 6.64 us -> none  [the longest x39 4.39 us: advance(): height[1:-1]]
    unnamed x10, local copies, waits for them, and re-layouts: 1.26 us -> 5.83 us
    concatenate x16 -> x0, other arithmetic: 2.49 us -> none  [with_halo(): jnp.concatenate([lax.ppermute(tail, axis, [(i, (i + 1) % count) for i in...]
  transfers between devices with their start and end apart: 60 -> 0, of which waited for: 58 -> 0; matrix products, arithmetic and copies ran while one was open for 1% -> 0% of each run, Pallas kernels for 0% -> 0%
where the time goes in v1:
time: 65 us; the launch traced here: 64.7 us
  Pallas kernels  58.2 us (90%)
  local copies, waits for them, and re-layouts  5.83 us (9%)
  between operations  0.65 us (1%)
    pallas_call x1, Pallas kernels, kernel_body(): pl.pallas_call(cycle_kernel, out_shape=(jax.ShapeDtypeStruct(tide_forcing...  58.2 us
    unnamed x10, local copies, waits for them, and re-layouts  5.83 us

profile of v1, /device:TPU:0, one launch (start us, length us, event | category | flops | bytes accessed | tf_op | source)
XLA Modules:
  0.0 64.7 jit_solution(891149491986193413)
XLA Ops:
  0.6 0.0 copy-start
  0.6 1.4 %copy-done = f32[8,3,16,1024]{3,2,1,0:T(8,128)S(1)} copy-done((f32[8,3,16,1024]{3,2,1,0:T(8,128)S(1)}, f32[8,3,16,1024]{3,2,1,0:T(8,128)}, u32[]{:S(2)}) %copy-start) | copy-done | bytes 1572888
  2.0 0.0 copy-start.1
  2.0 0.9 %copy-done.1 = f32[1,3,16,1024]{3,2,1,0:T(8,128)S(1)} copy-done((f32[1,3,16,1024]{3,2,1,0:T(8,128)S(1)}, f32[1,3,16,1024]{3,2,1,0:T(8,128)}, u32[]{:S(2)}) %copy-start.1) | copy-done | bytes 196632
  3.0 0.0 copy-start.2
  3.0 0.8 %copy-done.2 = f32[16,1024]{1,0:T(8,128)S(1)} copy-done((f32[16,1024]{1,0:T(8,128)S(1)}, f32[16,1024]{1,0:T(8,128)}, u32[]{:S(2)}) %copy-start.2) | copy-done | bytes 65560
  3.8 0.0 copy-start.3
  3.8 0.8 %copy-done.3 = f32[16,1024]{1,0:T(8,128)S(1)} copy-done((f32[16,1024]{1,0:T(8,128)S(1)}, f32[16,1024]{1,0:T(8,128)}, u32[]{:S(2)}) %copy-start.3) | copy-done | bytes 65560
  4.6 58.2 %shard_map.59 = (f32[8,3,16,1024]{3,2,1,0:T(8,128)S(1)}, f32[1,3,16,1024]{3,2,1,0:T(8,128)S(1)}) custom-call(f32[1,3,16,1024]{3,2,1,0:T(8,128)S(1)} %copy-done.1, f32[8,3,16,1024]{3,2,1,0:T(8,128)S(1)} %copy-done, f32[16,1024]{1,0:T(8,128)S(1)} %copy-done.2, f32[16,1024]{1,0:T(8,128)S(1)} %copy-done.3), custom_call_target="tpu_custom_call" | custom-call | tf_op jit(solution)/shard_map/pallas_call | solution.py:436
  62.9 1.1 %copy.8 = f32[8,3,16,1024]{3,2,1,0:T(8,128)} copy(f32[8,3,16,1024]{3,2,1,0:T(8,128)S(1)} %get-tuple-element.4) | data formatting | bytes 3145728
  64.0 0.7 %copy.9 = f32[1,3,16,1024]{3,2,1,0:T(8,128)} copy(f32[1,3,16,1024]{3,2,1,0:T(8,128)S(1)} %get-tuple-element.5) | data formatting | bytes 393216
Async XLA Ops:
  0.6 1.4 %copy-start = (f32[8,3,16,1024]{3,2,1,0:T(8,128)S(1)}, f32[8,3,16,1024]{3,2,1,0:T(8,128)}, u32[]{:S(2)}) copy-start(f32[8,3,16,1024]{3,2,1,0:T(8,128)} %forcing.1) | copy-start | bytes 4718596
  2.0 0.9 %copy-start.1 = (f32[1,3,16,1024]{3,2,1,0:T(8,128)S(1)}, f32[1,3,16,1024]{3,2,1,0:T(8,128)}, u32[]{:S(2)}) copy-start(f32[1,3,16,1024]{3,2,1,0:T(8,128)} %guess.1) | copy-start | bytes 589828
  3.0 0.8 %copy-start.2 = (f32[16,1024]{1,0:T(8,128)S(1)}, f32[16,1024]{1,0:T(8,128)}, u32[]{:S(2)}) copy-start(f32[16,1024]{1,0:T(8,128)} %depth.1) | copy-start | bytes 196612
  3.8 0.8 %copy-start.3 = (f32[16,1024]{1,0:T(8,128)S(1)}, f32[16,1024]{1,0:T(8,128)}, u32[]{:S(2)}) copy-start(f32[16,1024]{1,0:T(8,128)} %drag.1) | copy-start | bytes 196612

commit v2 on v1

--- a/solution.py
+++ b/solution.py
@@ -120,17 +120,29 @@
 
 
 def cycle_kernel(
-    guess, forcing, depth, drag, out, residual,
-    coef, track, mid, edges, edges_in, ahead, ahead_in, first, second, third, fourth,
-    climb, final, final_in, residual_in, relax, wave,
+    guess_hbm, forcing_hbm, depth_hbm, drag_hbm, out, residual,
+    guess, forcing, depth, drag, coef, track, mid, edges, edges_in, ahead, ahead_in, first, second, third, fourth,
+    climb, lower_in, lower_sum, climb_in, residual_in, relax, wave,
     coef_sems, edge_send, edge_recv, ahead_sems, res_send, res_recv,
     first_sems, second_sems, third_sems, fourth_send, fourth_recv, relay_send,
-    sibling_sems, final_sems,
+    sibling_sems, climb_sems, lower_sems, load_sems,
 ):
     tm = lax.axis_index("tm")
     sp = lax.axis_index("space")
     count = lax.axis_size("tm")
     moments = forcing.shape[0]
+    loads = [
+        pltpu.make_async_copy(src, dst, load_sems.at[index])
+        for index, (src, dst) in enumerate((
+            (depth_hbm, depth),
+            (drag_hbm, drag),
+            (guess_hbm, guess),
+            (forcing_hbm.at[0], forcing.at[0]),
+            (forcing_hbm.at[1:moments], forcing.at[1:moments]),
+        ))
+    ]
+    for load in loads:
+        load.start()
     own = guess.shape[2]
     rows = 2 * own
     cols = guess.shape[3]
@@ -217,6 +229,8 @@
     def coarse(src, dst):
         substep(src, dst, coarse_courant)
 
+    for load in loads[:4]:
+        load.wait()
     coef[0, 0:own] = 0.5 * depth[...]
     coef[1, 0:own] = 1.0 - drag[...]
     track[0, :, 0:own] = guess[0]
@@ -239,6 +253,7 @@
         )
 
     upper = lax.broadcasted_iota(jnp.int32, (3, own // 2, cols), 1) < 4
+    loads[4].wait()
     coef_copy.wait()
 
     def propagate(moment, carry):
@@ -285,6 +300,9 @@
 
         lax.fori_loop(low, high, step, 0)
 
+    lower_copy = remote(
+        first.at[0], lower_in, lower_sems.at[0], lower_sems.at[1], (tm, other)
+    )
     second_copy = remote(
         second.at[chip], second.at[chip], second_sems.at[0], second_sems.at[1], (facing, sp)
     )
@@ -317,6 +335,7 @@
         coarse(first.at[0], second.at[chip])
         second[chip] += first[1]
         second_copy.start()
+        lower_copy.start()
 
     res_here.start()
     res_there.start()
@@ -372,20 +391,14 @@
         rise(pair, climb.at[0], climb.at[1], third.at[0])
         rise(chip, climb.at[1], climb.at[0], second.at[0])
 
-    sibling = remote(climb.at[0], final, sibling_sems.at[0], sibling_sems.at[1], (before, sp))
-
-    @pl.when(odd == 1)
-    def _():
-        sibling.start()
-        coarse(climb.at[0], final)
-        final[...] += first[0]
-
-    @pl.when(odd == 0)
-    def _():
-        sibling.wait_recv()
-
-    final_copy = remote(final, final_in, final_sems.at[0], final_sems.at[1], (tm, other))
-    final_copy.start()
+    climb_copy = remote(
+        climb.at[0], climb_in, climb_sems.at[0], climb_sems.at[1], (tm, other)
+    )
+    sibling = remote(climb.at[1], wave.at[0], sibling_sems.at[0], sibling_sems.at[1], (before, sp))
+
+    @pl.when(odd == 1)
+    def _():
+        climb_copy.start()
 
     res_here.wait()
     res_there.wait()
@@ -399,17 +412,31 @@
     def _():
         second_copy.wait_send()
         third_copy.wait_send()
-        sibling.wait_send()
-
         @pl.when(inner)
         def _():
             for field in range(3):
                 gather(field, inward).wait_send()
                 relay(field, outward).wait_send()
 
-    final_copy.wait()
-    wave[0, :, 0:own] = final[:, 0:own] + final_in[:, own:rows]
-    wave[0, :, own:rows] = final[:, own:rows] + final_in[:, 0:own]
+    def combine(dst, kept, arrived):
+        dst[:, 0:own] = kept[:, 0:own] + arrived[:, own:rows]
+        dst[:, own:rows] = kept[:, own:rows] + arrived[:, 0:own]
+
+    @pl.when(odd == 1)
+    def _():
+        lower_copy.wait()
+        combine(lower_sum, first.at[0], lower_in)
+        climb_copy.wait()
+        combine(climb.at[1], climb.at[0], climb_in)
+        sibling.start()
+        coarse(climb.at[1], wave.at[0])
+        wave[0] += lower_sum[...]
+        sibling.wait_send()
+
+    @pl.when(odd == 0)
+    def _():
+        sibling.wait_recv()
+
     out[0] = guess[0] + wave[0, :, 0:own]
 
     def correct(moment, carry):
@@ -439,9 +466,13 @@
             jax.ShapeDtypeStruct(tide_forcing.shape, jnp.float32),
             jax.ShapeDtypeStruct(cpoint_guess.shape, jnp.float32),
         ),
-        in_specs=[vmem] * 4,
+        in_specs=[pl.BlockSpec(memory_space=pl.ANY)] * 4,
         out_specs=(vmem, vmem),
         scratch_shapes=[
+            held(*cpoint_guess.shape),
+            held(*tide_forcing.shape),
+            held(*depth.shape),
+            held(*drag.shape),
             held(2, 2 * own, cols),
             held(moments, *block),
             held(*block),
@@ -456,6 +487,7 @@
             held(2, *block),
             held(*block),
             held(*block),
+            held(*block),
             held(2, *part),
             held(2, *block),
             held(2, *block),
@@ -473,9 +505,11 @@
             dma((3,)),
             dma((2,)),
             dma((2,)),
+            dma((2,)),
+            dma((5,)),
         ],
         compiler_params=pltpu.CompilerParams(
-            collective_id=0, has_side_effects=True, vmem_limit_bytes=48 * 1024 * 1024
+            collective_id=0, has_side_effects=True, vmem_limit_bytes=60 * 1024 * 1024
         ),
     )(cpoint_guess, tide_forcing, depth, drag)
 

time: 65 us -> 60.3 us (0.928)
  local copies, waits for them, and re-layouts: 5.83 us -> 3.45 us
  Pallas kernels: 58.2 us -> 56 us
    unnamed x10 -> x4, local copies, waits for them, and re-layouts: 5.83 us -> 3.45 us
    pallas_call x1, Pallas kernels: 58.2 us -> 56 us  [kernel_body(): pl.pallas_call(cycle_kernel, out_shape=(jax.ShapeDtypeStruct(tide_forcing...]
where the time goes in v2:
time: 60.3 us; the launch traced here: 60.1 us
  Pallas kernels  56 us (93%)
  local copies, waits for them, and re-layouts  3.45 us (6%)
  between operations  0.65 us (1%)
    pallas_call x1, Pallas kernels, kernel_body(): pl.pallas_call(cycle_kernel, out_shape=(jax.ShapeDtypeStruct(tide_forcing...  56 us
    unnamed x4, local copies, waits for them, and re-layouts  3.45 us

profile of v2, /device:TPU:0, one launch (start us, length us, event | category | flops | bytes accessed | tf_op | source)
XLA Modules:
  0.0 60.1 jit_solution(1677620539970495082)
XLA Ops:
  0.6 56.0 %shard_map.59 = (f32[8,3,16,1024]{3,2,1,0:T(8,128)}, f32[1,3,16,1024]{3,2,1,0:T(8,128)}) custom-call(f32[1,3,16,1024]{3,2,1,0:T(8,128)} %guess_hbm.1, f32[8,3,16,1024]{3,2,1,0:T(8,128)} %forcing_hbm.1, f32[16,1024]{1,0:T(8,128)} %depth_hbm.1, f32[16,1024]{1,0:T(8,128)} %drag_hbm.1), custom_call_target="tpu_custom_call" | custom-call | tf_op jit(solution)/shard_map/pallas_call | solution.py:463
  56.7 0.0 copy-start
  56.7 2.8 %copy.8 = f32[8,3,16,1024]{3,2,1,0:T(8,128)} copy(f32[8,3,16,1024]{3,2,1,0:T(8,128)} %get-tuple-element.4) | data formatting | bytes 3145728
  59.4 0.0 copy-done
  59.4 0.7 %copy.9 = f32[1,3,16,1024]{3,2,1,0:T(8,128)} copy(f32[1,3,16,1024]{3,2,1,0:T(8,128)S(1)} %copy-done) | data formatting | bytes 393216
Async XLA Ops:
  56.7 2.8 %copy-start = (f32[1,3,16,1024]{3,2,1,0:T(8,128)S(1)}, f32[1,3,16,1024]{3,2,1,0:T(8,128)}, u32[]{:S(2)}) copy-start(f32[1,3,16,1024]{3,2,1,0:T(8,128)} %get-tuple-element.5) | copy-start | bytes 589828

commit v3 on v2

--- a/solution.py
+++ b/solution.py
@@ -170,7 +170,7 @@
 
     barrier = pltpu.get_barrier_semaphore()
     partners = [
-        (tm, other), (before, sp), (after, sp), (before, other), (after, other),
+        (tm, other), (before, sp), (after, sp),
         (facing, sp), ((tm + 4) % count, sp), ((tm + count - 4) % count, sp),
     ]
     for to in partners:
@@ -278,12 +278,11 @@
     def _():
         first_copy.start()
 
-    res_here = remote(
-        first.at[odd, :, 0:own], residual_in.at[0], res_send.at[0], res_recv.at[0], (after, sp)
-    )
-    res_there = remote(
-        first.at[odd, :, own:rows], residual_in.at[1], res_send.at[1], res_recv.at[1],
-        (after, other),
+    res_across = remote(
+        first.at[odd, :, own:rows], residual_in.at[0], res_send.at[0], res_recv.at[0], (tm, other)
+    )
+    res_onward = remote(
+        residual_in.at[1], residual_in.at[2], res_send.at[1], res_recv.at[1], (after, sp)
     )
 
     def relaxed(low, high):
@@ -337,8 +336,7 @@
         second_copy.start()
         lower_copy.start()
 
-    res_here.start()
-    res_there.start()
+    res_across.start()
     relaxed(1, 3)
 
     @pl.when(odd == 1)
@@ -400,9 +398,9 @@
     def _():
         climb_copy.start()
 
-    res_here.wait()
-    res_there.wait()
-    residual[0] = residual_in[0] + residual_in[1]
+    res_across.wait()
+    residual_in[1] = first[odd, :, 0:own] + residual_in[0]
+    res_onward.start()
 
     @pl.when(odd == 0)
     def _():
@@ -447,6 +445,8 @@
         return carry
 
     lax.fori_loop(1, moments, correct, 0)
+    res_onward.wait()
+    residual[0] = residual_in[2]
 
 
 def kernel_body(cpoint_guess, tide_forcing, depth, drag):
@@ -466,7 +466,7 @@
             jax.ShapeDtypeStruct(tide_forcing.shape, jnp.float32),
             jax.ShapeDtypeStruct(cpoint_guess.shape, jnp.float32),
         ),
-        in_specs=[pl.BlockSpec(memory_space=pl.ANY)] * 4,
+        in_specs=[pl.BlockSpec(memory_space=pltpu.HBM)] * 4,
         out_specs=(vmem, vmem),
         scratch_shapes=[
             held(*cpoint_guess.shape),
@@ -488,7 +488,7 @@
             held(*block),
             held(*block),
             held(*block),
-            held(2, *part),
+            held(3, *part),
             held(2, *block),
             held(2, *block),
             dma((2,)),
@@ -509,7 +509,7 @@
             dma((5,)),
         ],
         compiler_params=pltpu.CompilerParams(
-            collective_id=0, has_side_effects=True, vmem_limit_bytes=60 * 1024 * 1024
+            collective_id=0, has_side_effects=True, vmem_limit_bytes=40 * 1024 * 1024
         ),
     )(cpoint_guess, tide_forcing, depth, drag)
 

time: 60.3 us -> 58.2 us (0.965)
  Pallas kernels: 56 us -> 51.5 us
  local copies, waits for them, and re-layouts: 3.45 us -> 5.83 us
    pallas_call x1, Pallas kernels: 56 us -> 51.5 us  [kernel_body(): pl.pallas_call(cycle_kernel, out_shape=(jax.ShapeDtypeStruct(tide_forcing...]
    unnamed x4 -> x10, local copies, waits for them, and re-layouts: 3.45 us -> 5.83 us
where the time goes in v3:
time: 58.2 us; the launch traced here: 58 us
  Pallas kernels  51.5 us (88%)
  local copies, waits for them, and re-layouts  5.83 us (10%)
  between operations  0.65 us (1%)
    pallas_call x1, Pallas kernels, kernel_body(): pl.pallas_call(cycle_kernel, out_shape=(jax.ShapeDtypeStruct(tide_forcing...  51.5 us
    unnamed x10, local copies, waits for them, and re-layouts  5.83 us

profile of v3, /device:TPU:0, one launch (start us, length us, event | category | flops | bytes accessed | tf_op | source)
XLA Modules:
  0.0 58.0 jit_solution(4072844315325380048)
XLA Ops:
  0.6 0.0 copy-start
  0.6 1.4 %copy-done = f32[8,3,16,1024]{3,2,1,0:T(8,128)S(1)} copy-done((f32[8,3,16,1024]{3,2,1,0:T(8,128)S(1)}, f32[8,3,16,1024]{3,2,1,0:T(8,128)}, u32[]{:S(2)}) %copy-start) | copy-done | bytes 1572888
  2.0 0.0 copy-start.1
  2.0 0.9 %copy-done.1 = f32[1,3,16,1024]{3,2,1,0:T(8,128)S(1)} copy-done((f32[1,3,16,1024]{3,2,1,0:T(8,128)S(1)}, f32[1,3,16,1024]{3,2,1,0:T(8,128)}, u32[]{:S(2)}) %copy-start.1) | copy-done | bytes 196632
  3.0 0.0 copy-start.2
  3.0 0.8 %copy-done.2 = f32[16,1024]{1,0:T(8,128)S(1)} copy-done((f32[16,1024]{1,0:T(8,128)S(1)}, f32[16,1024]{1,0:T(8,128)}, u32[]{:S(2)}) %copy-start.2) | copy-done | bytes 65560
  3.8 0.0 copy-start.3
  3.8 0.8 %copy-done.3 = f32[16,1024]{1,0:T(8,128)S(1)} copy-done((f32[16,1024]{1,0:T(8,128)S(1)}, f32[16,1024]{1,0:T(8,128)}, u32[]{:S(2)}) %copy-start.3) | copy-done | bytes 65560
  4.6 51.5 %shard_map.59 = (f32[8,3,16,1024]{3,2,1,0:T(8,128)S(1)}, f32[1,3,16,1024]{3,2,1,0:T(8,128)S(1)}) custom-call(f32[1,3,16,1024]{3,2,1,0:T(8,128)S(1)} %copy-done.1, f32[8,3,16,1024]{3,2,1,0:T(8,128)S(1)} %copy-done, f32[16,1024]{1,0:T(8,128)S(1)} %copy-done.2, f32[16,1024]{1,0:T(8,128)S(1)} %copy-done.3), custom_call_target="tpu_custom_call" | custom-call | tf_op jit(solution)/shard_map/pallas_call | solution.py:463
  56.1 1.1 %copy.8 = f32[8,3,16,1024]{3,2,1,0:T(8,128)} copy(f32[8,3,16,1024]{3,2,1,0:T(8,128)S(1)} %get-tuple-element.4) | data formatting | bytes 3145728
  57.3 0.7 %copy.9 = f32[1,3,16,1024]{3,2,1,0:T(8,128)} copy(f32[1,3,16,1024]{3,2,1,0:T(8,128)S(1)} %get-tuple-element.5) | data formatting | bytes 393216
Async XLA Ops:
  0.6 1.4 %copy-start = (f32[8,3,16,1024]{3,2,1,0:T(8,128)S(1)}, f32[8,3,16,1024]{3,2,1,0:T(8,128)}, u32[]{:S(2)}) copy-start(f32[8,3,16,1024]{3,2,1,0:T(8,128)} %forcing_hbm.1) | copy-start | bytes 4718596
  2.0 0.9 %copy-start.1 = (f32[1,3,16,1024]{3,2,1,0:T(8,128)S(1)}, f32[1,3,16,1024]{3,2,1,0:T(8,128)}, u32[]{:S(2)}) copy-start(f32[1,3,16,1024]{3,2,1,0:T(8,128)} %guess_hbm.1) | copy-start | bytes 589828
  3.0 0.8 %copy-start.2 = (f32[16,1024]{1,0:T(8,128)S(1)}, f32[16,1024]{1,0:T(8,128)}, u32[]{:S(2)}) copy-start(f32[16,1024]{1,0:T(8,128)} %depth_hbm.1) | copy-start | bytes 196612
  3.8 0.8 %copy-start.3 = (f32[16,1024]{1,0:T(8,128)S(1)}, f32[16,1024]{1,0:T(8,128)}, u32[]{:S(2)}) copy-start(f32[16,1024]{1,0:T(8,128)} %drag_hbm.1) | copy-start | bytes 196612

commit v4 on v3

--- a/solution.py
+++ b/solution.py
@@ -509,7 +509,7 @@
             dma((5,)),
         ],
         compiler_params=pltpu.CompilerParams(
-            collective_id=0, has_side_effects=True, vmem_limit_bytes=40 * 1024 * 1024
+            collective_id=0, has_side_effects=True, vmem_limit_bytes=51 * 1024 * 1024
         ),
     )(cpoint_guess, tide_forcing, depth, drag)
 

time: 58.2 us -> 56.4 us (0.969)
  local copies, waits for them, and re-layouts: 5.83 us -> 4.42 us
    unnamed x10 -> x8, local copies, waits for them, and re-layouts: 5.83 us -> 4.42 us
where the time goes in v4:
time: 56.4 us; the launch traced here: 56.1 us
  Pallas kernels  51.1 us (91%)
  local copies, waits for them, and re-layouts  4.42 us (8%)
  between operations  0.65 us (1%)
    pallas_call x1, Pallas kernels, kernel_body(): pl.pallas_call(cycle_kernel, out_shape=(jax.ShapeDtypeStruct(tide_forcing...  51.1 us
    unnamed x8, local copies, waits for them, and re-layouts  4.42 us

profile of v4, /device:TPU:0, one launch (start us, length us, event | category | flops | bytes accessed | tf_op | source)
XLA Modules:
  0.0 56.1 jit_solution(8612166376749418000)
XLA Ops:
  0.6 0.0 copy-start
  0.6 0.9 %copy-done = f32[1,3,16,1024]{3,2,1,0:T(8,128)S(1)} copy-done((f32[1,3,16,1024]{3,2,1,0:T(8,128)S(1)}, f32[1,3,16,1024]{3,2,1,0:T(8,128)}, u32[]{:S(2)}) %copy-start) | copy-done | bytes 196632
  1.6 0.0 copy-start.1
  1.6 0.8 %copy-done.1 = f32[16,1024]{1,0:T(8,128)S(1)} copy-done((f32[16,1024]{1,0:T(8,128)S(1)}, f32[16,1024]{1,0:T(8,128)}, u32[]{:S(2)}) %copy-start.1) | copy-done | bytes 65560
  2.4 0.0 copy-start.2
  2.4 0.8 %copy-done.2 = f32[16,1024]{1,0:T(8,128)S(1)} copy-done((f32[16,1024]{1,0:T(8,128)S(1)}, f32[16,1024]{1,0:T(8,128)}, u32[]{:S(2)}) %copy-start.2) | copy-done | bytes 65560
  3.2 51.1 %shard_map.59 = (f32[8,3,16,1024]{3,2,1,0:T(8,128)S(1)}, f32[1,3,16,1024]{3,2,1,0:T(8,128)S(1)}) custom-call(f32[1,3,16,1024]{3,2,1,0:T(8,128)S(1)} %copy-done, f32[8,3,16,1024]{3,2,1,0:T(8,128)} %forcing_hbm.1, f32[16,1024]{1,0:T(8,128)S(1)} %copy-done.1, f32[16,1024]{1,0:T(8,128)S(1)} %copy-done.2), custom_call_target="tpu_custom_call" | custom-call | tf_op jit(solution)/shard_map/pallas_call | solution.py:463
  54.3 1.1 %copy.8 = f32[8,3,16,1024]{3,2,1,0:T(8,128)} copy(f32[8,3,16,1024]{3,2,1,0:T(8,128)S(1)} %get-tuple-element.4) | data formatting | bytes 3145728
  55.4 0.7 %copy.9 = f32[1,3,16,1024]{3,2,1,0:T(8,128)} copy(f32[1,3,16,1024]{3,2,1,0:T(8,128)S(1)} %get-tuple-element.5) | data formatting | bytes 393216
Async XLA Ops:
  0.6 0.9 %copy-start = (f32[1,3,16,1024]{3,2,1,0:T(8,128)S(1)}, f32[1,3,16,1024]{3,2,1,0:T(8,128)}, u32[]{:S(2)}) copy-start(f32[1,3,16,1024]{3,2,1,0:T(8,128)} %guess_hbm.1) | copy-start | bytes 589828
  1.6 0.8 %copy-start.1 = (f32[16,1024]{1,0:T(8,128)S(1)}, f32[16,1024]{1,0:T(8,128)}, u32[]{:S(2)}) copy-start(f32[16,1024]{1,0:T(8,128)} %depth_hbm.1) | copy-start | bytes 196612
  2.4 0.8 %copy-start.2 = (f32[16,1024]{1,0:T(8,128)S(1)}, f32[16,1024]{1,0:T(8,128)}, u32[]{:S(2)}) copy-start(f32[16,1024]{1,0:T(8,128)} %drag_hbm.1) | copy-start | bytes 196612
